TPU v7x, 256 devices: a whole 4x4x8 slice. The times are simulated.
256 devices in a mesh: leaf: 64 (over y, z, core), grid: 4 (over x).
Axes of the slice: x: 4, y: 4, z: 8, core: 2. Of those that a mesh axis runs over, the one named last changes fastest.
Arguments:
- rhs: bfloat16 [5, 128, 256, 256], P(None, 'leaf', 'grid'), may hold values from -6 to 6
- fwd_inv: bfloat16 [5, 128, 256, 256], P(None, 'leaf', 'grid')
- bwd_inv: bfloat16 [5, 128, 256, 256], P(None, 'leaf', 'grid')
- upd_t: bfloat16 [4, 128, 256, 512], P(None, 'leaf', 'grid'), may hold values from -0.25 to 0.25
- bwd_t: bfloat16 [4, 128, 512, 256], P(None, 'leaf', 'grid'), may hold values from -0.1875 to 0.1875
- dest_owner: int32 [4, 64, 4, 256, 1], P(None, 'leaf', 'grid'), may hold values from 0 to 63; in each aligned block of 256 rows (0 to 255, 256 to 511, ..., all dimensions but the last counted through in order) at most 10 rows name the same one
- dest_row: int32 [4, 64, 4, 256], P(None, 'leaf', 'grid'), may hold values from 128 to 639, as said below
Outputs:
- solution: bfloat16 [5, 128, 256, 256], P(None, 'leaf', 'grid')
Inputs may be any that keep to these rules, and one draw needn't show every extreme that they name: `dest_owner`: in the rows of one device at one level (one aligned block of 256), no owner is named more than 10 times, a bound that some block reaches. `dest_row`: an entry of level l reaches a row of a later level: it lies from (l + 1) * 2 * 64 to 639.
All inputs are finite; a program needn't handle non-finite values.
Results may differ from a plain program's by a relative error of at most 0.025.
Values may be sent and summed in bfloat16 or wider, within the bound.
A program may use at most 64 MiB of HBM per device.

v0:
```python
import jax
import jax.numpy as jnp
from jax import lax
from jax.sharding import PartitionSpec as P


def apply_inverse(inverse_rows, block_bf):
    return jnp.einsum(
        "kiw,kwn->kin",
        inverse_rows,
        lax.all_gather(block_bf, "grid", axis=1, tiled=True),
        preferred_element_type=jnp.float32,
    )


def grid_reduce(term_fn, kept_rows):
    return lax.psum_scatter(
        term_fn(jnp.int32(0), kept_rows * lax.axis_size("grid")).astype(jnp.bfloat16),
        "grid",
        scatter_dimension=0,
        tiled=True,
    ).astype(jnp.float32)


def send_back(solved_rows):
    return lax.all_to_all(solved_rows, "leaf", split_axis=0, concat_axis=0, tiled=True)


def local(rhs, fwd_inv, bwd_inv, upd_t, bwd_t, dest_owner, dest_row):
    levels, per_level, grid_rows, columns = rhs.shape
    group_rows = bwd_t.shape[2]
    owners = lax.axis_size("leaf")
    capacity = max(2, 8 * per_level * group_rows // (3 * owners))
    block_rows = per_level * grid_rows
    leaf_ids = jnp.arange(owners, dtype=jnp.int32)
    accum = rhs.astype(jnp.float32).reshape(levels * block_rows, columns)

    def placement(level):
        owner_ids = dest_owner[level].reshape(-1)
        targets = dest_row[level].reshape(-1)
        onehot = (owner_ids[:, None] == leaf_ids[None, :]).astype(jnp.int32)
        before = jnp.cumsum(onehot, axis=0) - onehot
        slot_in = jnp.sum(before * onehot, axis=1)
        return (owner_ids * capacity + slot_in, targets)

    forward_out = []
    kept_index = []
    for level in range(levels):
        block = accum[level * block_rows : (level + 1) * block_rows].reshape(
            per_level, grid_rows, columns
        )
        block_bf = block.astype(jnp.bfloat16)
        solved = apply_inverse(fwd_inv[level], block_bf)
        forward_out.append(solved)
        if level < levels - 1:
            lowered = solved.astype(jnp.bfloat16)

            def forward_term(offset, length, lower_cols=upd_t[level], lowered=lowered):
                return jnp.einsum(
                    "kwr,kwn->rkn", lower_cols, lowered, preferred_element_type=jnp.float32
                )

            summed = grid_reduce(forward_term, group_rows)
            routed = summed.reshape(group_rows * per_level, columns)
            slot_pos, targets = placement(level)
            outgoing = jnp.zeros((owners * capacity, columns), jnp.float32).at[slot_pos].set(routed)
            outgoing_index = jnp.zeros((owners * capacity,), jnp.int32).at[slot_pos].set(targets)
            incoming, incoming_index = (
                lax.all_to_all(
                    outgoing.reshape(owners, capacity, columns).astype(jnp.bfloat16),
                    "leaf",
                    split_axis=0,
                    concat_axis=0,
                    tiled=True,
                ).astype(jnp.float32),
                lax.all_to_all(
                    outgoing_index.reshape(owners, capacity),
                    "leaf",
                    split_axis=0,
                    concat_axis=0,
                    tiled=True,
                ),
            )
            accum = accum.at[incoming_index.reshape(-1)].add(-incoming.reshape(-1, columns))
            kept_index.append(incoming_index)
    solution = jnp.zeros((levels * block_rows, columns), jnp.bfloat16)
    for level in reversed(range(levels)):
        reduced = forward_out[level]
        if level < levels - 1:
            slot_pos, targets = placement(level)
            asking = (
                jnp.zeros((owners * capacity,), jnp.int32)
                .at[slot_pos]
                .set(targets)
                .reshape(owners, capacity)
            )

            def answer(asked, solution=solution):
                found = solution[asked.reshape(-1)].reshape(asked.shape[0], asked.shape[1], columns)
                return send_back(found)

            returned = answer(
                lax.all_to_all(asking, "leaf", split_axis=0, concat_axis=0, tiled=True)
            )
            pulled = returned.reshape(owners * capacity, columns)[slot_pos].reshape(
                group_rows, per_level, columns
            )

            def backward_term(offset, length, upper_rows=bwd_t[level], pulled=pulled):
                return jnp.einsum(
                    "kjw,jkn->wkn", upper_rows, pulled, preferred_element_type=jnp.float32
                )

            upper_sum = grid_reduce(backward_term, grid_rows)
            reduced = reduced - jnp.swapaxes(upper_sum, 0, 1)
        result = apply_inverse(bwd_inv[level], reduced.astype(jnp.bfloat16))
        solution = solution.at[level * block_rows : (level + 1) * block_rows].set(
            result.astype(jnp.bfloat16).reshape(block_rows, columns)
        )
    return solution.reshape(levels, per_level, grid_rows, columns)


def solution(mesh):
    placed = (
        P(None, "leaf", "grid", None),
        P(None, "leaf", "grid", None),
        P(None, "leaf", "grid", None),
        P(None, "leaf", "grid", None),
        P(None, "leaf", "grid", None),
        P(None, "leaf", "grid", None, None),
        P(None, "leaf", "grid", None),
    )
    return jax.shard_map(
        local, mesh=mesh, in_specs=placed, out_specs=P(None, "leaf", "grid", None), check_vma=False
    )
```

profile of v0, /device:TPU:8, one launch (start us, length us, event | category | flops | bytes accessed | tf_op | source)
XLA Modules:
  0.0 601.4 jit_solution(17086478699634533320)
XLA Ops:
  7.4 12.6 %all-gather = bf16[1,2,256,256]{3,2,1,0:T(8,128)(2,1)S(1)} all-gather(bf16[1,2,64,256]{3,2,1,0:T(8,128)(2,1)S(1)} %slice-done), channel_id=2, replica_groups=mesh['leaf'=64,'grid'=4] {'grid'}, dimensions={2}, use_global_device_ids=true | all-gather | bytes 327680 | tf_op jit(solution)/shard_map/all_gather | solution.py:11
  33.2 12.1 %all-to-all-start = ((s32[64,1,10]{2,1,0:T(1,128)}), s32[64,1,10]{2,1,0:T(1,128)S(1)}, u32[]{:S(2)}, u32[]{:S(2)}) async-start(s32[64,1,10]{2,1,0:T(1,128)} %bitcast.8), calls=%async_computation | async-start | bytes 65536 | tf_op jit(solution)/shard_map/all_to_all | solution.py:76
  45.4 3.6 reduce-scatter.25.cloned.1.call-done
  50.4 1.6 scatter_custom_fusion.1
  53.9 9.7 %all-to-all-start.1 = ((bf16[64,10,256]{2,1,0:T(8,128)(2,1)}), bf16[64,10,256]{2,1,0:T(8,128)(2,1)S(1)}, u32[]{:S(2)}, u32[]{:S(2)}) async-start(bf16[64,10,256]{2,1,0:T(8,128)(2,1)} %convert_element_type.212), calls=%async_computation.1 | async-start | bytes 1048576 | tf_op jit(solution)/shard_map/all_to_all | solution.py:69
  65.1 15.1 %all-to-all-done.1 = bf16[64,10,256]{2,1,0:T(8,128)(2,1)S(1)} async-done(((bf16[64,10,256]{2,1,0:T(8,128)(2,1)}), bf16[64,10,256]{2,1,0:T(8,128)(2,1)S(1)}, u32[]{:S(2)}, u32[]{:S(2)}) %all-to-all-start.1) | async-done | bytes 327712 | tf_op jit(solution)/shard_map/all_to_all | solution.py:69
  80.5 6.3 %scatter_fusion = f32[640,256]{1,0:T(8,128)S(1)} fusion(f32[640,256]{1,0:T(8,128)S(1)} %bitcast_convert_fusion, s32[640]{0:T(1024)S(1)} %fusion.79, f32[640,256]{1,0:T(8,128)S(1)} %reshape.692), kind=kCustom, calls=%fused_computation.10 | custom fusion | flops 163840 | bytes 1968640 | tf_op jit(solution)/shard_map/scatter-add | solution.py:84
  86.9 12.5 %all_gather.31 = bf16[2,256,256]{2,1,0:T(8,128)(2,1)S(1)} all-gather(bf16[2,64,256]{2,1,0:T(8,128)(2,1)S(1)} %bitcast.266), channel_id=1, replica_groups=mesh['leaf'=64,'grid'=4] {'grid'}, dimensions={1}, use_global_device_ids=true | all-gather | bytes 327680 | tf_op jit(solution)/shard_map/all_gather | solution.py:11
  103.9 7.2 %all-to-all-start.2 = ((s32[64,1,10]{2,1,0:T(1,128)}), s32[64,1,10]{2,1,0:T(1,128)S(1)}, u32[]{:S(2)}, u32[]{:S(2)}) async-start(s32[64,1,10]{2,1,0:T(1,128)} %bitcast.20), calls=%async_computation.2 | async-start | bytes 65536 | tf_op jit(solution)/shard_map/all_to_all | solution.py:76
  111.1 11.1 %reduce-scatter.27.cloned.1.call-done = bf16[128,512]{1,0:T(8,128)(2,1)} async-done(((bf16[512,512]{1,0:T(8,128)(2,1)}), bf16[128,512]{1,0:T(8,128)(2,1)}) %reduce-scatter.27.cloned.1.call-update) | async-done | bytes 131088
  126.0 10.7 %all-to-all-start.3 = ((bf16[64,10,256]{2,1,0:T(8,128)(2,1)}), bf16[64,10,256]{2,1,0:T(8,128)(2,1)S(1)}, u32[]{:S(2)}, u32[]{:S(2)}) async-start(bf16[64,10,256]{2,1,0:T(8,128)(2,1)} %convert_element_type.221), calls=%async_computation.3 | async-start | bytes 1048576 | tf_op jit(solution)/shard_map/all_to_all | solution.py:69
  137.6 15.7 %all-to-all-done.3 = bf16[64,10,256]{2,1,0:T(8,128)(2,1)S(1)} async-done(((bf16[64,10,256]{2,1,0:T(8,128)(2,1)}), bf16[64,10,256]{2,1,0:T(8,128)(2,1)S(1)}, u32[]{:S(2)}, u32[]{:S(2)}) %all-to-all-start.3) | async-done | bytes 327712 | tf_op jit(solution)/shard_map/all_to_all | solution.py:69
  153.6 6.3 %scatter_fusion.1 = f32[640,256]{1,0:T(8,128)S(1)} fusion(f32[640,256]{1,0:T(8,128)S(1)} %scatter_fusion, s32[640]{0:T(1024)S(1)} %fusion.80, f32[640,256]{1,0:T(8,128)S(1)} %reshape.716), kind=kCustom, calls=%fused_computation.13 | custom fusion | flops 163840 | bytes 1968640 | tf_op jit(solution)/shard_map/scatter-add | solution.py:84
  160.0 12.4 %all_gather.32 = bf16[2,256,256]{2,1,0:T(8,128)(2,1)S(1)} all-gather(bf16[2,64,256]{2,1,0:T(8,128)(2,1)S(1)} %bitcast.267), channel_id=1, replica_groups=mesh['leaf'=64,'grid'=4] {'grid'}, dimensions={1}, use_global_device_ids=true | all-gather | bytes 327680 | tf_op jit(solution)/shard_map/all_gather | solution.py:11
  176.9 7.0 %all-to-all-start.4 = ((s32[64,1,10]{2,1,0:T(1,128)}), s32[64,1,10]{2,1,0:T(1,128)S(1)}, u32[]{:S(2)}, u32[]{:S(2)}) async-start(s32[64,1,10]{2,1,0:T(1,128)} %bitcast.33), calls=%async_computation.4 | async-start | bytes 65536 | tf_op jit(solution)/shard_map/all_to_all | solution.py:76
  184.0 11.2 %reduce-scatter.29.cloned.1.call-done = bf16[128,512]{1,0:T(8,128)(2,1)} async-done(((bf16[512,512]{1,0:T(8,128)(2,1)}), bf16[128,512]{1,0:T(8,128)(2,1)}) %reduce-scatter.29.cloned.1.call-update) | async-done | bytes 131088
  199.1 10.7 %all-to-all-start.5 = ((bf16[64,10,256]{2,1,0:T(8,128)(2,1)}), bf16[64,10,256]{2,1,0:T(8,128)(2,1)S(1)}, u32[]{:S(2)}, u32[]{:S(2)}) async-start(bf16[64,10,256]{2,1,0:T(8,128)(2,1)} %convert_element_type.230), calls=%async_computation.5 | async-start | bytes 1048576 | tf_op jit(solution)/shard_map/all_to_all | solution.py:69
  211.2 15.3 %all-to-all-done.5 = bf16[64,10,256]{2,1,0:T(8,128)(2,1)S(1)} async-done(((bf16[64,10,256]{2,1,0:T(8,128)(2,1)}), bf16[64,10,256]{2,1,0:T(8,128)(2,1)S(1)}, u32[]{:S(2)}, u32[]{:S(2)}) %all-to-all-start.5) | async-done | bytes 327712 | tf_op jit(solution)/shard_map/all_to_all | solution.py:69
  226.7 6.3 %scatter_fusion.2 = f32[640,256]{1,0:T(8,128)S(1)} fusion(f32[640,256]{1,0:T(8,128)S(1)} %scatter_fusion.1, s32[640]{0:T(1024)S(1)} %fusion.81, f32[640,256]{1,0:T(8,128)S(1)} %reshape.740), kind=kCustom, calls=%fused_computation.16 | custom fusion | flops 163840 | bytes 1968640 | tf_op jit(solution)/shard_map/scatter-add | solution.py:84
  233.1 12.4 %all_gather.33 = bf16[2,256,256]{2,1,0:T(8,128)(2,1)S(1)} all-gather(bf16[2,64,256]{2,1,0:T(8,128)(2,1)S(1)} %bitcast.268), channel_id=1, replica_groups=mesh['leaf'=64,'grid'=4] {'grid'}, dimensions={1}, use_global_device_ids=true | all-gather | bytes 327680 | tf_op jit(solution)/shard_map/all_gather | solution.py:11
  250.1 7.0 %all-to-all-start.6 = ((s32[64,1,10]{2,1,0:T(1,128)}), s32[64,1,10]{2,1,0:T(1,128)S(1)}, u32[]{:S(2)}, u32[]{:S(2)}) async-start(s32[64,1,10]{2,1,0:T(1,128)} %bitcast.46), calls=%async_computation.6 | async-start | bytes 65536 | tf_op jit(solution)/shard_map/all_to_all | solution.py:76
  257.1 11.3 %reduce-scatter.31.cloned.1.call-done = bf16[128,512]{1,0:T(8,128)(2,1)} async-done(((bf16[512,512]{1,0:T(8,128)(2,1)}), bf16[128,512]{1,0:T(8,128)(2,1)}) %reduce-scatter.31.cloned.1.call-update) | async-done | bytes 131088
  269.7 1.6 scatter_custom_fusion.10
  272.3 10.7 %all-to-all-start.7 = ((bf16[64,10,256]{2,1,0:T(8,128)(2,1)}), bf16[64,10,256]{2,1,0:T(8,128)(2,1)S(1)}, u32[]{:S(2)}, u32[]{:S(2)}) async-start(bf16[64,10,256]{2,1,0:T(8,128)(2,1)} %convert_element_type.239), calls=%async_computation.7 | async-start | bytes 1048576 | tf_op jit(solution)/shard_map/all_to_all | solution.py:69
  283.8 15.8 %all-to-all-done.7 = bf16[64,10,256]{2,1,0:T(8,128)(2,1)S(1)} async-done(((bf16[64,10,256]{2,1,0:T(8,128)(2,1)}), bf16[64,10,256]{2,1,0:T(8,128)(2,1)S(1)}, u32[]{:S(2)}, u32[]{:S(2)}) %all-to-all-start.7) | async-done | bytes 327712 | tf_op jit(solution)/shard_map/all_to_all | solution.py:69
  299.9 6.3 %scatter_fusion.3 = f32[640,256]{1,0:T(8,128)S(1)} fusion(f32[640,256]{1,0:T(8,128)S(1)} %scatter_fusion.2, s32[640]{0:T(1024)S(1)} %fusion.82, f32[640,256]{1,0:T(8,128)S(1)} %reshape.764), kind=kCustom, calls=%fused_computation.19 | custom fusion | flops 163840 | bytes 1968640 | tf_op jit(solution)/shard_map/scatter-add | solution.py:84
  306.2 12.6 %all_gather.34 = bf16[2,256,256]{2,1,0:T(8,128)(2,1)S(1)} all-gather(bf16[2,64,256]{2,1,0:T(8,128)(2,1)S(1)} %bitcast.265), channel_id=1, replica_groups=mesh['leaf'=64,'grid'=4] {'grid'}, dimensions={1}, use_global_device_ids=true | all-gather | bytes 327680 | tf_op jit(solution)/shard_map/all_gather | solution.py:11
  319.9 12.3 %all_gather.35 = bf16[2,256,256]{2,1,0:T(8,128)(2,1)S(1)} all-gather(bf16[2,64,256]{2,1,0:T(8,128)(2,1)S(1)} %fusion.4), channel_id=1, replica_groups=mesh['leaf'=64,'grid'=4] {'grid'}, dimensions={1}, use_global_device_ids=true | all-gather | bytes 327680 | tf_op jit(solution)/shard_map/all_gather | solution.py:11
  332.4 2.8 gather_fusion
  336.0 7.2 %all-to-all-start.8 = ((bf16[64,10,256]{2,1,0:T(8,128)(2,1)}), bf16[64,10,256]{2,1,0:T(8,128)(2,1)S(1)}, u32[]{:S(2)}, u32[]{:S(2)}) async-start(bf16[64,10,256]{2,1,0:T(8,128)(2,1)} %reshape.581), calls=%async_computation.8 | async-start | bytes 1048576 | tf_op jit(solution)/shard_map/all_to_all | solution.py:26
  343.3 16.6 %all-to-all-done.8 = bf16[64,10,256]{2,1,0:T(8,128)(2,1)S(1)} async-done(((bf16[64,10,256]{2,1,0:T(8,128)(2,1)}), bf16[64,10,256]{2,1,0:T(8,128)(2,1)S(1)}, u32[]{:S(2)}, u32[]{:S(2)}) %all-to-all-start.8) | async-done | bytes 327712 | tf_op jit(solution)/shard_map/all_to_all | solution.py:26
  362.3 19.6 %reduce-scatter.17.cloned.1.call-done = bf16[64,2,256]{2,0,1:T(8,128)(2,1)} async-done(((bf16[256,2,256]{2,0,1:T(8,128)(2,1)}), bf16[64,2,256]{2,0,1:T(8,128)(2,1)}) %reduce-scatter.17.cloned.1.call-update) | async-done | bytes 65552 | tf_op jit(solution)/shard_map/reduce_scatter | solution.py:17
  382.7 12.3 %all_gather.36 = bf16[2,256,256]{2,1,0:T(8,128)(2,1)S(1)} all-gather(bf16[2,64,256]{2,1,0:T(8,128)(2,1)S(1)} %fusion.21), channel_id=1, replica_groups=mesh['leaf'=64,'grid'=4] {'grid'}, dimensions={1}, use_global_device_ids=true | all-gather | bytes 327680 | tf_op jit(solution)/shard_map/all_gather | solution.py:11
  395.2 2.8 gather_fusion.2
  398.9 10.6 %all-to-all-start.9 = ((bf16[64,10,256]{2,1,0:T(8,128)(2,1)}), bf16[64,10,256]{2,1,0:T(8,128)(2,1)S(1)}, u32[]{:S(2)}, u32[]{:S(2)}) async-start(bf16[64,10,256]{2,1,0:T(8,128)(2,1)} %reshape.585), calls=%async_computation.10 | async-start | bytes 1048576 | tf_op jit(solution)/shard_map/all_to_all | solution.py:26
  409.5 16.6 %all-to-all-done.9 = bf16[64,10,256]{2,1,0:T(8,128)(2,1)S(1)} async-done(((bf16[64,10,256]{2,1,0:T(8,128)(2,1)}), bf16[64,10,256]{2,1,0:T(8,128)(2,1)S(1)}, u32[]{:S(2)}, u32[]{:S(2)}) %all-to-all-start.9) | async-done | bytes 327712 | tf_op jit(solution)/shard_map/all_to_all | solution.py:26
  428.5 19.6 %reduce-scatter.19.cloned.1.call-done = bf16[64,2,256]{2,0,1:T(8,128)(2,1)} async-done(((bf16[256,2,256]{2,0,1:T(8,128)(2,1)}), bf16[64,2,256]{2,0,1:T(8,128)(2,1)}) %reduce-scatter.19.cloned.1.call-update) | async-done | bytes 65552 | tf_op jit(solution)/shard_map/reduce_scatter | solution.py:17
  448.9 12.3 %all_gather.37 = bf16[2,256,256]{2,1,0:T(8,128)(2,1)S(1)} all-gather(bf16[2,64,256]{2,1,0:T(8,128)(2,1)S(1)} %fusion.19), channel_id=1, replica_groups=mesh['leaf'=64,'grid'=4] {'grid'}, dimensions={1}, use_global_device_ids=true | all-gather | bytes 327680 | tf_op jit(solution)/shard_map/all_gather | solution.py:11
  461.3 2.8 gather_fusion.4
  465.0 10.6 %all-to-all-start.10 = ((bf16[64,10,256]{2,1,0:T(8,128)(2,1)}), bf16[64,10,256]{2,1,0:T(8,128)(2,1)S(1)}, u32[]{:S(2)}, u32[]{:S(2)}) async-start(bf16[64,10,256]{2,1,0:T(8,128)(2,1)} %reshape.589), calls=%async_computation.12 | async-start | bytes 1048576 | tf_op jit(solution)/shard_map/all_to_all | solution.py:26
  475.7 16.6 %all-to-all-done.10 = bf16[64,10,256]{2,1,0:T(8,128)(2,1)S(1)} async-done(((bf16[64,10,256]{2,1,0:T(8,128)(2,1)}), bf16[64,10,256]{2,1,0:T(8,128)(2,1)S(1)}, u32[]{:S(2)}, u32[]{:S(2)}) %all-to-all-start.10) | async-done | bytes 327712 | tf_op jit(solution)/shard_map/all_to_all | solution.py:26
  494.6 19.6 %reduce-scatter.21.cloned.1.call-done = bf16[64,2,256]{2,0,1:T(8,128)(2,1)} async-done(((bf16[256,2,256]{2,0,1:T(8,128)(2,1)}), bf16[64,2,256]{2,0,1:T(8,128)(2,1)}) %reduce-scatter.21.cloned.1.call-update) | async-done | bytes 65552 | tf_op jit(solution)/shard_map/reduce_scatter | solution.py:17
  515.1 12.3 %all_gather.38 = bf16[2,256,256]{2,1,0:T(8,128)(2,1)S(1)} all-gather(bf16[2,64,256]{2,1,0:T(8,128)(2,1)S(1)} %fusion.17), channel_id=1, replica_groups=mesh['leaf'=64,'grid'=4] {'grid'}, dimensions={1}, use_global_device_ids=true | all-gather | bytes 327680 | tf_op jit(solution)/shard_map/all_gather | solution.py:11
  527.5 2.8 gather_fusion.6
  531.2 10.6 %all-to-all-start.11 = ((bf16[64,10,256]{2,1,0:T(8,128)(2,1)}), bf16[64,10,256]{2,1,0:T(8,128)(2,1)S(1)}, u32[]{:S(2)}, u32[]{:S(2)}) async-start(bf16[64,10,256]{2,1,0:T(8,128)(2,1)} %reshape.593), calls=%async_computation.14 | async-start | bytes 1048576 | tf_op jit(solution)/shard_map/all_to_all | solution.py:26
  541.8 16.6 %all-to-all-done.11 = bf16[64,10,256]{2,1,0:T(8,128)(2,1)S(1)} async-done(((bf16[64,10,256]{2,1,0:T(8,128)(2,1)}), bf16[64,10,256]{2,1,0:T(8,128)(2,1)S(1)}, u32[]{:S(2)}, u32[]{:S(2)}) %all-to-all-start.11) | async-done | bytes 327712 | tf_op jit(solution)/shard_map/all_to_all | solution.py:26
  560.8 19.6 %reduce-scatter.23.cloned.1.call-done = bf16[64,2,256]{2,0,1:T(8,128)(2,1)} async-done(((bf16[256,2,256]{2,0,1:T(8,128)(2,1)}), bf16[64,2,256]{2,0,1:T(8,128)(2,1)}) %reduce-scatter.23.cloned.1.call-update) | async-done | bytes 65552 | tf_op jit(solution)/shard_map/reduce_scatter | solution.py:17
  581.2 12.3 %all_gather.39 = bf16[2,256,256]{2,1,0:T(8,128)(2,1)S(1)} all-gather(bf16[2,64,256]{2,1,0:T(8,128)(2,1)S(1)} %fusion.15), channel_id=1, replica_groups=mesh['leaf'=64,'grid'=4] {'grid'}, dimensions={1}, use_global_device_ids=true | all-gather | bytes 327680 | tf_op jit(solution)/shard_map/all_gather | solution.py:11
  (186 shorter events, 65.5 us)
Async XLA Ops:
  6.5 0.8 slice-start
  6.5 14.4 %copy-start.1 = (bf16[4,2,64,512]{3,2,1,0:T(8,128)(2,1)S(1)}, bf16[4,2,64,512]{3,2,1,0:T(8,128)(2,1)}, u32[]{:S(2)}) copy-start(bf16[4,2,64,512]{3,2,1,0:T(8,128)(2,1)} %param.20) | copy-start | bytes 1572868
  6.5 42.5 %reduce-scatter.25.cloned.1.call-start = ((), (), s32[]{:S(2)}) async-start(), calls=%async_computation.24 | async-start | bytes 655360
  22.3 0.7 copy-start.5
  25.5 0.6 copy-start.6
  26.1 0.6 copy-start.7
  26.7 0.6 copy-start.8
  27.5 0.6 copy-start.9
  27.5 0.7 slice-start.1
  28.2 0.6 slice-start.2
  29.0 0.7 slice-start.3
  29.8 0.6 slice-start.4
  30.4 0.7 copy-start.10
  33.2 20.7 %all-to-all-start = ((s32[64,1,10]{2,1,0:T(1,128)}), s32[64,1,10]{2,1,0:T(1,128)S(1)}, u32[]{:S(2)}, u32[]{:S(2)}) async-start(s32[64,1,10]{2,1,0:T(1,128)} %bitcast.8), calls=%async_computation | async-start | bytes 65536 | tf_op jit(solution)/shard_map/all_to_all | solution.py:76
  52.9 10.8 %copy-start.3 = (bf16[5,2,64,256]{3,2,1,0:T(8,128)(2,1)S(1)}, bf16[5,2,64,256]{3,2,1,0:T(8,128)(2,1)}, u32[]{:S(2)}) copy-start(bf16[5,2,64,256]{3,2,1,0:T(8,128)(2,1)} %param.17) | copy-start | bytes 983044
  53.9 26.4 %all-to-all-start.1 = ((bf16[64,10,256]{2,1,0:T(8,128)(2,1)}), bf16[64,10,256]{2,1,0:T(8,128)(2,1)S(1)}, u32[]{:S(2)}, u32[]{:S(2)}) async-start(bf16[64,10,256]{2,1,0:T(8,128)(2,1)} %convert_element_type.212), calls=%async_computation.1 | async-start | bytes 1048576 | tf_op jit(solution)/shard_map/all_to_all | solution.py:69
  63.6 58.5 %reduce-scatter.27.cloned.1.call-start = ((), (), s32[]{:S(2)}) async-start(), calls=%async_computation.25 | async-start | bytes 655360
  103.9 22.2 %all-to-all-start.2 = ((s32[64,1,10]{2,1,0:T(1,128)}), s32[64,1,10]{2,1,0:T(1,128)S(1)}, u32[]{:S(2)}, u32[]{:S(2)}) async-start(s32[64,1,10]{2,1,0:T(1,128)} %bitcast.20), calls=%async_computation.2 | async-start | bytes 65536 | tf_op jit(solution)/shard_map/all_to_all | solution.py:76
  126.0 27.3 %all-to-all-start.3 = ((bf16[64,10,256]{2,1,0:T(8,128)(2,1)}), bf16[64,10,256]{2,1,0:T(8,128)(2,1)S(1)}, u32[]{:S(2)}, u32[]{:S(2)}) async-start(bf16[64,10,256]{2,1,0:T(8,128)(2,1)} %convert_element_type.221), calls=%async_computation.3 | async-start | bytes 1048576 | tf_op jit(solution)/shard_map/all_to_all | solution.py:69
  136.7 58.5 %reduce-scatter.29.cloned.1.call-start = ((), (), s32[]{:S(2)}) async-start(), calls=%async_computation.26 | async-start | bytes 655360
  176.9 22.2 %all-to-all-start.4 = ((s32[64,1,10]{2,1,0:T(1,128)}), s32[64,1,10]{2,1,0:T(1,128)S(1)}, u32[]{:S(2)}, u32[]{:S(2)}) async-start(s32[64,1,10]{2,1,0:T(1,128)} %bitcast.33), calls=%async_computation.4 | async-start | bytes 65536 | tf_op jit(solution)/shard_map/all_to_all | solution.py:76
  199.1 27.4 %all-to-all-start.5 = ((bf16[64,10,256]{2,1,0:T(8,128)(2,1)}), bf16[64,10,256]{2,1,0:T(8,128)(2,1)S(1)}, u32[]{:S(2)}, u32[]{:S(2)}) async-start(bf16[64,10,256]{2,1,0:T(8,128)(2,1)} %convert_element_type.230), calls=%async_computation.5 | async-start | bytes 1048576 | tf_op jit(solution)/shard_map/all_to_all | solution.py:69
  209.8 58.5 %reduce-scatter.31.cloned.1.call-start = ((), (), s32[]{:S(2)}) async-start(), calls=%async_computation.27 | async-start | bytes 655360
  250.1 22.2 %all-to-all-start.6 = ((s32[64,1,10]{2,1,0:T(1,128)}), s32[64,1,10]{2,1,0:T(1,128)S(1)}, u32[]{:S(2)}, u32[]{:S(2)}) async-start(s32[64,1,10]{2,1,0:T(1,128)} %bitcast.46), calls=%async_computation.6 | async-start | bytes 65536 | tf_op jit(solution)/shard_map/all_to_all | solution.py:76
  272.3 27.4 %all-to-all-start.7 = ((bf16[64,10,256]{2,1,0:T(8,128)(2,1)}), bf16[64,10,256]{2,1,0:T(8,128)(2,1)S(1)}, u32[]{:S(2)}, u32[]{:S(2)}) async-start(bf16[64,10,256]{2,1,0:T(8,128)(2,1)} %convert_element_type.239), calls=%async_computation.7 | async-start | bytes 1048576 | tf_op jit(solution)/shard_map/all_to_all | solution.py:69
  318.8 13.3 %copy-start.4 = (bf16[5,2,64,256]{3,2,1,0:T(8,128)(2,1)S(1)}, bf16[5,2,64,256]{3,2,1,0:T(8,128)(2,1)}, u32[]{:S(2)}) copy-start(bf16[5,2,64,256]{3,2,1,0:T(8,128)(2,1)} %param.19) | copy-start | bytes 983044
  336.0 23.8 %all-to-all-start.8 = ((bf16[64,10,256]{2,1,0:T(8,128)(2,1)}), bf16[64,10,256]{2,1,0:T(8,128)(2,1)S(1)}, u32[]{:S(2)}, u32[]{:S(2)}) async-start(bf16[64,10,256]{2,1,0:T(8,128)(2,1)} %reshape.581), calls=%async_computation.8 | async-start | bytes 1048576 | tf_op jit(solution)/shard_map/all_to_all | solution.py:26
  343.2 38.7 %reduce-scatter.17.cloned.1.call-start = ((), (), s32[]{:S(2)}) async-start(), calls=%async_computation.20 | async-start | bytes 327680 | tf_op jit(solution)/shard_map/reduce_scatter | solution.py:17
  360.0 1.2 copy-start.2
  398.9 27.2 %all-to-all-start.9 = ((bf16[64,10,256]{2,1,0:T(8,128)(2,1)}), bf16[64,10,256]{2,1,0:T(8,128)(2,1)S(1)}, u32[]{:S(2)}, u32[]{:S(2)}) async-start(bf16[64,10,256]{2,1,0:T(8,128)(2,1)} %reshape.585), calls=%async_computation.10 | async-start | bytes 1048576 | tf_op jit(solution)/shard_map/all_to_all | solution.py:26
  409.4 38.6 %reduce-scatter.19.cloned.1.call-start = ((), (), s32[]{:S(2)}) async-start(), calls=%async_computation.21 | async-start | bytes 327680 | tf_op jit(solution)/shard_map/reduce_scatter | solution.py:17
  465.0 27.2 %all-to-all-start.10 = ((bf16[64,10,256]{2,1,0:T(8,128)(2,1)}), bf16[64,10,256]{2,1,0:T(8,128)(2,1)S(1)}, u32[]{:S(2)}, u32[]{:S(2)}) async-start(bf16[64,10,256]{2,1,0:T(8,128)(2,1)} %reshape.589), calls=%async_computation.12 | async-start | bytes 1048576 | tf_op jit(solution)/shard_map/all_to_all | solution.py:26
  475.6 38.6 %reduce-scatter.21.cloned.1.call-start = ((), (), s32[]{:S(2)}) async-start(), calls=%async_computation.22 | async-start | bytes 327680 | tf_op jit(solution)/shard_map/reduce_scatter | solution.py:17
  531.2 27.2 %all-to-all-start.11 = ((bf16[64,10,256]{2,1,0:T(8,128)(2,1)}), bf16[64,10,256]{2,1,0:T(8,128)(2,1)S(1)}, u32[]{:S(2)}, u32[]{:S(2)}) async-start(bf16[64,10,256]{2,1,0:T(8,128)(2,1)} %reshape.593), calls=%async_computation.14 | async-start | bytes 1048576 | tf_op jit(solution)/shard_map/all_to_all | solution.py:26
  541.8 38.6 %reduce-scatter.23.cloned.1.call-start = ((), (), s32[]{:S(2)}) async-start(), calls=%async_computation.23 | async-start | bytes 327680 | tf_op jit(solution)/shard_map/reduce_scatter | solution.py:17
  593.7 0.7 copy-start
Sparse Core Ops, SparseCore 0:
  22.5 26.4 reduce-scatter.24
  101.8 20.2 reduce-scatter.26
  174.9 20.2 reduce-scatter.28
  248.0 20.2 reduce-scatter.30
  362.4 19.4 reduce-scatter.16
  428.6 19.4 reduce-scatter.18
  494.7 19.4 reduce-scatter.20
  560.9 19.4 reduce-scatter.22
where the time goes:
time: 611 us; the launch traced here: 601 us
  waiting for transfers between devices  245 us (40%)
  blocking collectives  124 us (20%)
  starting transfers between devices  115 us (19%)
  local copies, waits for them, and re-layouts  56.7 us (9%)
  other arithmetic  35.3 us (6%)
  between operations  14.5 us (2%)
  matrix products  11.2 us (2%)
    all_gather x10, blocking collectives, apply_inverse(): lax.all_gather(block_bf, 'grid', axis=1, tiled=True)  124 us
    reduce_scatter x4, waiting for transfers between devices, grid_reduce(): lax.psum_scatter(term_fn(jnp.int32(0), kept_rows * lax.axis_size('grid'))...  78.4 us
    all_to_all x4, waiting for transfers between devices, send_back(): lax.all_to_all(solved_rows, 'leaf', split_axis=0, concat_axis=0, tiled=True)  66.4 us
    all_to_all x4, waiting for transfers between devices, local(): lax.all_to_all(outgoing.reshape(owners, capacity, columns).astype(jnp.bfl...  62 us
    all_to_all x4, starting transfers between devices, local(): lax.all_to_all(outgoing.reshape(owners, capacity, columns).astype(jnp.bfl...  41.7 us
    all_to_all x4, starting transfers between devices, send_back(): lax.all_to_all(solved_rows, 'leaf', split_axis=0, concat_axis=0, tiled=True)  38.8 us
    unnamed x12, waiting for transfers between devices  37.3 us
    all_to_all x4, starting transfers between devices, local(): lax.all_to_all(outgoing_index.reshape(owners, capacity), 'leaf', split_ax...  33.4 us
  transfers between devices with their start and end apart: 20, of which 17 were waited for; matrix products, arithmetic and copies ran while one was open for 5% of the time, Pallas kernels for 0%

commit v1 on v0

--- a/solution.py
+++ b/solution.py
@@ -5,10 +5,18 @@
 
 
 def apply_inverse(inverse_rows, block_bf):
+
+    def view_the_record(inner_x, axis_id):
+        base_arr = jnp.concatenate(
+            lax.all_to_all(jnp.stack(lax.axis_size(axis_id) * [inner_x], axis=0), axis_id, 0, 0),
+            axis=1,
+        )
+        return base_arr
+
     return jnp.einsum(
         "kiw,kwn->kin",
         inverse_rows,
-        lax.all_gather(block_bf, "grid", axis=1, tiled=True),
+        view_the_record(block_bf, "grid"),
         preferred_element_type=jnp.float32,
     )
 

time: 611 us -> 586 us (0.959)
  blocking collectives: 124 us -> 49.8 us
  waiting for transfers between devices: 245 us -> 275 us
  starting transfers between devices: 115 us -> 130 us
    all_gather x10 -> x0, blocking collectives: 124 us -> none  [apply_inverse(): lax.all_gather(block_bf, 'grid', axis=1, tiled=True)]
    all_to_all x0 -> x5, blocking collectives: none -> 49.8 us  [view_the_record(): lax.all_to_all(jnp.stack(lax.axis_size(axis_id) * [inner_x], axis=0), axi...]
    all_to_all x0 -> x5, waiting for transfers between devices: none -> 30.9 us  [view_the_record(): lax.all_to_all(jnp.stack(lax.axis_size(axis_id) * [inner_x], axis=0), axi...]
    all_to_all x0 -> x5, starting transfers between devices: none -> 18.1 us  [view_the_record(): lax.all_to_all(jnp.stack(lax.axis_size(axis_id) * [inner_x], axis=0), axi...]
  transfers between devices with their start and end apart: 20 -> 25, of which waited for: 17 -> 21; matrix products, arithmetic and copies ran while one was open for 5% -> 5% of each run, Pallas kernels for 0% -> 0%
where the time goes in v1:
time: 586 us; the launch traced here: 576 us
  waiting for transfers between devices  275 us (47%)
  starting transfers between devices  130 us (22%)
  local copies, waits for them, and re-layouts  59.9 us (10%)
  blocking collectives  49.8 us (8%)
  other arithmetic  35.3 us (6%)
  between operations  14.7 us (3%)
  matrix products  11.2 us (2%)
    reduce_scatter x4, waiting for transfers between devices, grid_reduce(): lax.psum_scatter(term_fn(jnp.int32(0), kept_rows * lax.axis_size('grid'))...  77.3 us
    all_to_all x4, waiting for transfers between devices, send_back(): lax.all_to_all(solved_rows, 'leaf', split_axis=0, concat_axis=0, tiled=True)  66.4 us
    all_to_all x4, waiting for transfers between devices, local(): lax.all_to_all(outgoing.reshape(owners, capacity, columns).astype(jnp.bfl...  62 us
    all_to_all x5, blocking collectives, view_the_record(): lax.all_to_all(jnp.stack(lax.axis_size(axis_id) * [inner_x], axis=0), axi...  49.8 us
    all_to_all x4, starting transfers between devices, local(): lax.all_to_all(outgoing.reshape(owners, capacity, columns).astype(jnp.bfl...  42.7 us
    unnamed x12, waiting for transfers between devices  38.1 us
    all_to_all x4, starting transfers between devices, send_back(): lax.all_to_all(solved_rows, 'leaf', split_axis=0, concat_axis=0, tiled=True)  37.9 us
    all_to_all x5, waiting for transfers between devices, view_the_record(): lax.all_to_all(jnp.stack(lax.axis_size(axis_id) * [inner_x], axis=0), axi...  30.9 us
  transfers between devices with their start and end apart: 25, of which 21 were waited for; matrix products, arithmetic and copies ran while one was open for 5% of the time, Pallas kernels for 0%

profile of v1, /device:TPU:8, one launch (start us, length us, event | category | flops | bytes accessed | tf_op | source)
XLA Modules:
  0.0 575.7 jit_solution(9912033154459736082)
XLA Ops:
  8.1 4.4 all-to-all-start.1
  14.8 4.4 all-to-all-done.1
  29.6 12.1 %all-to-all-start = ((s32[64,1,10]{2,1,0:T(1,128)}), s32[64,1,10]{2,1,0:T(1,128)S(1)}, u32[]{:S(2)}, u32[]{:S(2)}) async-start(s32[64,1,10]{2,1,0:T(1,128)} %bitcast.8), calls=%async_computation | async-start | bytes 65536 | tf_op jit(solution)/shard_map/all_to_all | solution.py:84
  41.7 5.3 reduce-scatter.25.cloned.1.call-done
  50.8 10.7 %all-to-all-start.2 = ((bf16[64,10,256]{2,1,0:T(8,128)(2,1)}), bf16[64,10,256]{2,1,0:T(8,128)(2,1)S(1)}, u32[]{:S(2)}, u32[]{:S(2)}) async-start(bf16[64,10,256]{2,1,0:T(8,128)(2,1)} %convert_element_type.217), calls=%async_computation.2 | async-start | bytes 1048576 | tf_op jit(solution)/shard_map/all_to_all | solution.py:77
  63.1 15.1 %all-to-all-done.2 = bf16[64,10,256]{2,1,0:T(8,128)(2,1)S(1)} async-done(((bf16[64,10,256]{2,1,0:T(8,128)(2,1)}), bf16[64,10,256]{2,1,0:T(8,128)(2,1)S(1)}, u32[]{:S(2)}, u32[]{:S(2)}) %all-to-all-start.2) | async-done | bytes 327712 | tf_op jit(solution)/shard_map/all_to_all | solution.py:77
  78.5 6.3 %scatter_fusion = f32[640,256]{1,0:T(8,128)S(1)} fusion(f32[640,256]{1,0:T(8,128)S(1)} %bitcast_convert_fusion, s32[640]{0:T(1024)S(1)} %fusion.78, f32[640,256]{1,0:T(8,128)S(1)} %reshape.794), kind=kCustom, calls=%fused_computation.10 | custom fusion | flops 163840 | bytes 1968640 | tf_op jit(solution)/shard_map/scatter-add | solution.py:92
  84.8 10.1 %all_to_all.130 = bf16[4,2,64,256]{3,2,1,0:T(8,128)(2,1)S(1)} all-to-all(bf16[4,2,64,256]{3,2,1,0:T(8,128)(2,1)S(1)} %stack.24), channel_id=1, replica_groups=mesh['leaf'=64,'grid'=4] {'grid'}, dimensions={0} | all-to-all | bytes 524288 | tf_op jit(solution)/shard_map/all_to_all | solution.py:11
  99.5 6.3 %all-to-all-start.3 = ((s32[64,1,10]{2,1,0:T(1,128)}), s32[64,1,10]{2,1,0:T(1,128)S(1)}, u32[]{:S(2)}, u32[]{:S(2)}) async-start(s32[64,1,10]{2,1,0:T(1,128)} %bitcast.22), calls=%async_computation.3 | async-start | bytes 65536 | tf_op jit(solution)/shard_map/all_to_all | solution.py:84
  105.9 10.8 %reduce-scatter.27.cloned.1.call-done = bf16[128,512]{1,0:T(8,128)(2,1)} async-done(((bf16[512,512]{1,0:T(8,128)(2,1)}), bf16[128,512]{1,0:T(8,128)(2,1)}) %reduce-scatter.27.cloned.1.call-update) | async-done | bytes 131088
  120.5 10.7 %all-to-all-start.5 = ((bf16[64,10,256]{2,1,0:T(8,128)(2,1)}), bf16[64,10,256]{2,1,0:T(8,128)(2,1)S(1)}, u32[]{:S(2)}, u32[]{:S(2)}) async-start(bf16[64,10,256]{2,1,0:T(8,128)(2,1)} %convert_element_type.226), calls=%async_computation.5 | async-start | bytes 1048576 | tf_op jit(solution)/shard_map/all_to_all | solution.py:77
  132.1 15.7 %all-to-all-done.5 = bf16[64,10,256]{2,1,0:T(8,128)(2,1)S(1)} async-done(((bf16[64,10,256]{2,1,0:T(8,128)(2,1)}), bf16[64,10,256]{2,1,0:T(8,128)(2,1)S(1)}, u32[]{:S(2)}, u32[]{:S(2)}) %all-to-all-start.5) | async-done | bytes 327712 | tf_op jit(solution)/shard_map/all_to_all | solution.py:77
  148.1 6.3 %scatter_fusion.1 = f32[640,256]{1,0:T(8,128)S(1)} fusion(f32[640,256]{1,0:T(8,128)S(1)} %scatter_fusion, s32[640]{0:T(1024)S(1)} %fusion.79, f32[640,256]{1,0:T(8,128)S(1)} %reshape.818), kind=kCustom, calls=%fused_computation.13 | custom fusion | flops 163840 | bytes 1968640 | tf_op jit(solution)/shard_map/scatter-add | solution.py:92
  154.5 10.1 %all_to_all.131 = bf16[4,2,64,256]{3,2,1,0:T(8,128)(2,1)S(1)} all-to-all(bf16[4,2,64,256]{3,2,1,0:T(8,128)(2,1)S(1)} %stack.25), channel_id=1, replica_groups=mesh['leaf'=64,'grid'=4] {'grid'}, dimensions={0} | all-to-all | bytes 524288 | tf_op jit(solution)/shard_map/all_to_all | solution.py:11
  169.2 6.2 %all-to-all-start.6 = ((s32[64,1,10]{2,1,0:T(1,128)}), s32[64,1,10]{2,1,0:T(1,128)S(1)}, u32[]{:S(2)}, u32[]{:S(2)}) async-start(s32[64,1,10]{2,1,0:T(1,128)} %bitcast.37), calls=%async_computation.6 | async-start | bytes 65536 | tf_op jit(solution)/shard_map/all_to_all | solution.py:84
  175.3 11.0 %reduce-scatter.29.cloned.1.call-done = bf16[128,512]{1,0:T(8,128)(2,1)} async-done(((bf16[512,512]{1,0:T(8,128)(2,1)}), bf16[128,512]{1,0:T(8,128)(2,1)}) %reduce-scatter.29.cloned.1.call-update) | async-done | bytes 131088
  190.2 10.7 %all-to-all-start.8 = ((bf16[64,10,256]{2,1,0:T(8,128)(2,1)}), bf16[64,10,256]{2,1,0:T(8,128)(2,1)S(1)}, u32[]{:S(2)}, u32[]{:S(2)}) async-start(bf16[64,10,256]{2,1,0:T(8,128)(2,1)} %convert_element_type.235), calls=%async_computation.8 | async-start | bytes 1048576 | tf_op jit(solution)/shard_map/all_to_all | solution.py:77
  202.2 15.3 %all-to-all-done.8 = bf16[64,10,256]{2,1,0:T(8,128)(2,1)S(1)} async-done(((bf16[64,10,256]{2,1,0:T(8,128)(2,1)}), bf16[64,10,256]{2,1,0:T(8,128)(2,1)S(1)}, u32[]{:S(2)}, u32[]{:S(2)}) %all-to-all-start.8) | async-done | bytes 327712 | tf_op jit(solution)/shard_map/all_to_all | solution.py:77
  217.8 6.3 %scatter_fusion.2 = f32[640,256]{1,0:T(8,128)S(1)} fusion(f32[640,256]{1,0:T(8,128)S(1)} %scatter_fusion.1, s32[640]{0:T(1024)S(1)} %fusion.80, f32[640,256]{1,0:T(8,128)S(1)} %reshape.842), kind=kCustom, calls=%fused_computation.16 | custom fusion | flops 163840 | bytes 1968640 | tf_op jit(solution)/shard_map/scatter-add | solution.py:92
  224.1 10.1 %all_to_all.132 = bf16[4,2,64,256]{3,2,1,0:T(8,128)(2,1)S(1)} all-to-all(bf16[4,2,64,256]{3,2,1,0:T(8,128)(2,1)S(1)} %stack.26), channel_id=1, replica_groups=mesh['leaf'=64,'grid'=4] {'grid'}, dimensions={0} | all-to-all | bytes 524288 | tf_op jit(solution)/shard_map/all_to_all | solution.py:11
  238.8 6.1 %all-to-all-start.9 = ((s32[64,1,10]{2,1,0:T(1,128)}), s32[64,1,10]{2,1,0:T(1,128)S(1)}, u32[]{:S(2)}, u32[]{:S(2)}) async-start(s32[64,1,10]{2,1,0:T(1,128)} %bitcast.52), calls=%async_computation.9 | async-start | bytes 65536 | tf_op jit(solution)/shard_map/all_to_all | solution.py:84
  245.0 11.0 %reduce-scatter.31.cloned.1.call-done = bf16[128,512]{1,0:T(8,128)(2,1)} async-done(((bf16[512,512]{1,0:T(8,128)(2,1)}), bf16[128,512]{1,0:T(8,128)(2,1)}) %reduce-scatter.31.cloned.1.call-update) | async-done | bytes 131088
  259.8 10.6 %all-to-all-start.11 = ((bf16[64,10,256]{2,1,0:T(8,128)(2,1)}), bf16[64,10,256]{2,1,0:T(8,128)(2,1)S(1)}, u32[]{:S(2)}, u32[]{:S(2)}) async-start(bf16[64,10,256]{2,1,0:T(8,128)(2,1)} %convert_element_type.244), calls=%async_computation.11 | async-start | bytes 1048576 | tf_op jit(solution)/shard_map/all_to_all | solution.py:77
  271.4 15.8 %all-to-all-done.11 = bf16[64,10,256]{2,1,0:T(8,128)(2,1)S(1)} async-done(((bf16[64,10,256]{2,1,0:T(8,128)(2,1)}), bf16[64,10,256]{2,1,0:T(8,128)(2,1)S(1)}, u32[]{:S(2)}, u32[]{:S(2)}) %all-to-all-start.11) | async-done | bytes 327712 | tf_op jit(solution)/shard_map/all_to_all | solution.py:77
  287.4 6.3 %scatter_fusion.3 = f32[640,256]{1,0:T(8,128)S(1)} fusion(f32[640,256]{1,0:T(8,128)S(1)} %scatter_fusion.2, s32[640]{0:T(1024)S(1)} %fusion.81, f32[640,256]{1,0:T(8,128)S(1)} %reshape.866), kind=kCustom, calls=%fused_computation.19 | custom fusion | flops 163840 | bytes 1968640 | tf_op jit(solution)/shard_map/scatter-add | solution.py:92
  293.8 10.3 %all_to_all.133 = bf16[4,2,64,256]{3,2,1,0:T(8,128)(2,1)S(1)} all-to-all(bf16[4,2,64,256]{3,2,1,0:T(8,128)(2,1)S(1)} %stack.27), channel_id=1, replica_groups=mesh['leaf'=64,'grid'=4] {'grid'}, dimensions={0} | all-to-all | bytes 524288 | tf_op jit(solution)/shard_map/all_to_all | solution.py:11
  305.8 3.4 all-to-all-start.13
  309.3 6.6 %all-to-all-done.13 = bf16[4,2,64,256]{3,2,1,0:T(8,128)(2,1)S(1)} async-done(((bf16[4,2,64,256]{3,2,1,0:T(8,128)(2,1)}), bf16[4,2,64,256]{3,2,1,0:T(8,128)(2,1)S(1)}, u32[]{:S(2)}, u32[]{:S(2)}) %all-to-all-start.13) | async-done | bytes 262176 | tf_op jit(solution)/shard_map/all_to_all | solution.py:11
  319.8 6.1 %all-to-all-start.14 = ((bf16[64,10,256]{2,1,0:T(8,128)(2,1)}), bf16[64,10,256]{2,1,0:T(8,128)(2,1)S(1)}, u32[]{:S(2)}, u32[]{:S(2)}) async-start(bf16[64,10,256]{2,1,0:T(8,128)(2,1)} %reshape.675), calls=%async_computation.14 | async-start | bytes 1048576 | tf_op jit(solution)/shard_map/all_to_all | solution.py:34
  326.0 16.6 %all-to-all-done.14 = bf16[64,10,256]{2,1,0:T(8,128)(2,1)S(1)} async-done(((bf16[64,10,256]{2,1,0:T(8,128)(2,1)}), bf16[64,10,256]{2,1,0:T(8,128)(2,1)S(1)}, u32[]{:S(2)}, u32[]{:S(2)}) %all-to-all-start.14) | async-done | bytes 327712 | tf_op jit(solution)/shard_map/all_to_all | solution.py:34
  345.0 19.3 %reduce-scatter.17.cloned.1.call-done = bf16[64,2,256]{2,0,1:T(8,128)(2,1)} async-done(((bf16[256,2,256]{2,0,1:T(8,128)(2,1)}), bf16[64,2,256]{2,0,1:T(8,128)(2,1)}) %reduce-scatter.17.cloned.1.call-update) | async-done | bytes 65552 | tf_op jit(solution)/shard_map/reduce_scatter | solution.py:25
  365.9 3.4 all-to-all-start.15
  369.3 6.6 %all-to-all-done.15 = bf16[4,2,64,256]{3,2,1,0:T(8,128)(2,1)S(1)} async-done(((bf16[4,2,64,256]{3,2,1,0:T(8,128)(2,1)}), bf16[4,2,64,256]{3,2,1,0:T(8,128)(2,1)S(1)}, u32[]{:S(2)}, u32[]{:S(2)}) %all-to-all-start.15) | async-done | bytes 262176 | tf_op jit(solution)/shard_map/all_to_all | solution.py:11
  379.8 10.6 %all-to-all-start.16 = ((bf16[64,10,256]{2,1,0:T(8,128)(2,1)}), bf16[64,10,256]{2,1,0:T(8,128)(2,1)S(1)}, u32[]{:S(2)}, u32[]{:S(2)}) async-start(bf16[64,10,256]{2,1,0:T(8,128)(2,1)} %reshape.681), calls=%async_computation.17 | async-start | bytes 1048576 | tf_op jit(solution)/shard_map/all_to_all | solution.py:34
  390.5 16.6 %all-to-all-done.16 = bf16[64,10,256]{2,1,0:T(8,128)(2,1)S(1)} async-done(((bf16[64,10,256]{2,1,0:T(8,128)(2,1)}), bf16[64,10,256]{2,1,0:T(8,128)(2,1)S(1)}, u32[]{:S(2)}, u32[]{:S(2)}) %all-to-all-start.16) | async-done | bytes 327712 | tf_op jit(solution)/shard_map/all_to_all | solution.py:34
  409.4 19.3 %reduce-scatter.19.cloned.1.call-done = bf16[64,2,256]{2,0,1:T(8,128)(2,1)} async-done(((bf16[256,2,256]{2,0,1:T(8,128)(2,1)}), bf16[64,2,256]{2,0,1:T(8,128)(2,1)}) %reduce-scatter.19.cloned.1.call-update) | async-done | bytes 65552 | tf_op jit(solution)/shard_map/reduce_scatter | solution.py:25
  430.3 3.4 all-to-all-start.17
  433.8 6.6 %all-to-all-done.17 = bf16[4,2,64,256]{3,2,1,0:T(8,128)(2,1)S(1)} async-done(((bf16[4,2,64,256]{3,2,1,0:T(8,128)(2,1)}), bf16[4,2,64,256]{3,2,1,0:T(8,128)(2,1)S(1)}, u32[]{:S(2)}, u32[]{:S(2)}) %all-to-all-start.17) | async-done | bytes 262176 | tf_op jit(solution)/shard_map/all_to_all | solution.py:11
  440.6 2.8 gather_fusion.4
  444.3 10.6 %all-to-all-start.18 = ((bf16[64,10,256]{2,1,0:T(8,128)(2,1)}), bf16[64,10,256]{2,1,0:T(8,128)(2,1)S(1)}, u32[]{:S(2)}, u32[]{:S(2)}) async-start(bf16[64,10,256]{2,1,0:T(8,128)(2,1)} %reshape.687), calls=%async_computation.20 | async-start | bytes 1048576 | tf_op jit(solution)/shard_map/all_to_all | solution.py:34
  454.9 16.6 %all-to-all-done.18 = bf16[64,10,256]{2,1,0:T(8,128)(2,1)S(1)} async-done(((bf16[64,10,256]{2,1,0:T(8,128)(2,1)}), bf16[64,10,256]{2,1,0:T(8,128)(2,1)S(1)}, u32[]{:S(2)}, u32[]{:S(2)}) %all-to-all-start.18) | async-done | bytes 327712 | tf_op jit(solution)/shard_map/all_to_all | solution.py:34
  473.9 19.3 %reduce-scatter.21.cloned.1.call-done = bf16[64,2,256]{2,0,1:T(8,128)(2,1)} async-done(((bf16[256,2,256]{2,0,1:T(8,128)(2,1)}), bf16[64,2,256]{2,0,1:T(8,128)(2,1)}) %reduce-scatter.21.cloned.1.call-update) | async-done | bytes 65552 | tf_op jit(solution)/shard_map/reduce_scatter | solution.py:25
  494.8 3.4 all-to-all-start.19
  498.2 6.6 %all-to-all-done.19 = bf16[4,2,64,256]{3,2,1,0:T(8,128)(2,1)S(1)} async-done(((bf16[4,2,64,256]{3,2,1,0:T(8,128)(2,1)}), bf16[4,2,64,256]{3,2,1,0:T(8,128)(2,1)S(1)}, u32[]{:S(2)}, u32[]{:S(2)}) %all-to-all-start.19) | async-done | bytes 262176 | tf_op jit(solution)/shard_map/all_to_all | solution.py:11
  508.7 10.6 %all-to-all-start.20 = ((bf16[64,10,256]{2,1,0:T(8,128)(2,1)}), bf16[64,10,256]{2,1,0:T(8,128)(2,1)S(1)}, u32[]{:S(2)}, u32[]{:S(2)}) async-start(bf16[64,10,256]{2,1,0:T(8,128)(2,1)} %reshape.693), calls=%async_computation.23 | async-start | bytes 1048576 | tf_op jit(solution)/shard_map/all_to_all | solution.py:34
  519.3 16.6 %all-to-all-done.20 = bf16[64,10,256]{2,1,0:T(8,128)(2,1)S(1)} async-done(((bf16[64,10,256]{2,1,0:T(8,128)(2,1)}), bf16[64,10,256]{2,1,0:T(8,128)(2,1)S(1)}, u32[]{:S(2)}, u32[]{:S(2)}) %all-to-all-start.20) | async-done | bytes 327712 | tf_op jit(solution)/shard_map/all_to_all | solution.py:34
  538.3 19.3 %reduce-scatter.23.cloned.1.call-done = bf16[64,2,256]{2,0,1:T(8,128)(2,1)} async-done(((bf16[256,2,256]{2,0,1:T(8,128)(2,1)}), bf16[64,2,256]{2,0,1:T(8,128)(2,1)}) %reduce-scatter.23.cloned.1.call-update) | async-done | bytes 65552 | tf_op jit(solution)/shard_map/reduce_scatter | solution.py:25
  558.5 9.2 %all_to_all.134 = bf16[4,2,64,256]{3,2,1,0:T(8,128)(2,1)S(1)} all-to-all(bf16[4,2,64,256]{3,2,1,0:T(8,128)(2,1)S(1)} %stack.32), channel_id=1, replica_groups=mesh['leaf'=64,'grid'=4] {'grid'}, dimensions={0} | all-to-all | bytes 524288 | tf_op jit(solution)/shard_map/all_to_all | solution.py:11
  (210 shorter events, 79.2 us)
Async XLA Ops:
  8.1 4.4 copy-start.5
  8.1 11.1 %all-to-all-start.1 = ((bf16[4,2,64,256]{3,2,1,0:T(8,128)(2,1)}), bf16[4,2,64,256]{3,2,1,0:T(8,128)(2,1)S(1)}, u32[]{:S(2)}, u32[]{:S(2)}) async-start(bf16[4,2,64,256]{3,2,1,0:T(8,128)(2,1)} %stack.23), calls=%async_computation.1 | async-start | bytes 524288 | tf_op jit(solution)/shard_map/all_to_all | solution.py:11
  12.5 34.4 %reduce-scatter.25.cloned.1.call-start = ((), (), s32[]{:S(2)}) async-start(), calls=%async_computation.34 | async-start | bytes 655360
  14.8 5.4 copy-start.1
  21.8 0.6 copy-start.6
  22.4 0.6 copy-start.7
  23.0 0.6 copy-start.8
  23.8 0.6 copy-start.9
  23.8 0.7 slice-start
  24.6 0.6 slice-start.1
  25.3 0.7 slice-start.2
  26.1 0.6 slice-start.3
  26.7 0.7 copy-start.10
  29.6 21.3 %all-to-all-start = ((s32[64,1,10]{2,1,0:T(1,128)}), s32[64,1,10]{2,1,0:T(1,128)S(1)}, u32[]{:S(2)}, u32[]{:S(2)}) async-start(s32[64,1,10]{2,1,0:T(1,128)} %bitcast.8), calls=%async_computation | async-start | bytes 65536 | tf_op jit(solution)/shard_map/all_to_all | solution.py:84
  50.8 10.8 %copy-start.3 = (bf16[5,2,64,256]{3,2,1,0:T(8,128)(2,1)S(1)}, bf16[5,2,64,256]{3,2,1,0:T(8,128)(2,1)}, u32[]{:S(2)}) copy-start(bf16[5,2,64,256]{3,2,1,0:T(8,128)(2,1)} %param.17) | copy-start | bytes 983044
  50.8 27.4 %all-to-all-start.2 = ((bf16[64,10,256]{2,1,0:T(8,128)(2,1)}), bf16[64,10,256]{2,1,0:T(8,128)(2,1)S(1)}, u32[]{:S(2)}, u32[]{:S(2)}) async-start(bf16[64,10,256]{2,1,0:T(8,128)(2,1)} %convert_element_type.217), calls=%async_computation.2 | async-start | bytes 1048576 | tf_op jit(solution)/shard_map/all_to_all | solution.py:77
  61.6 55.1 %reduce-scatter.27.cloned.1.call-start = ((), (), s32[]{:S(2)}) async-start(), calls=%async_computation.35 | async-start | bytes 655360
  99.5 21.0 %all-to-all-start.3 = ((s32[64,1,10]{2,1,0:T(1,128)}), s32[64,1,10]{2,1,0:T(1,128)S(1)}, u32[]{:S(2)}, u32[]{:S(2)}) async-start(s32[64,1,10]{2,1,0:T(1,128)} %bitcast.22), calls=%async_computation.3 | async-start | bytes 65536 | tf_op jit(solution)/shard_map/all_to_all | solution.py:84
  120.5 27.3 %all-to-all-start.5 = ((bf16[64,10,256]{2,1,0:T(8,128)(2,1)}), bf16[64,10,256]{2,1,0:T(8,128)(2,1)S(1)}, u32[]{:S(2)}, u32[]{:S(2)}) async-start(bf16[64,10,256]{2,1,0:T(8,128)(2,1)} %convert_element_type.226), calls=%async_computation.5 | async-start | bytes 1048576 | tf_op jit(solution)/shard_map/all_to_all | solution.py:77
  131.2 55.1 %reduce-scatter.29.cloned.1.call-start = ((), (), s32[]{:S(2)}) async-start(), calls=%async_computation.36 | async-start | bytes 655360
  169.2 21.0 %all-to-all-start.6 = ((s32[64,1,10]{2,1,0:T(1,128)}), s32[64,1,10]{2,1,0:T(1,128)S(1)}, u32[]{:S(2)}, u32[]{:S(2)}) async-start(s32[64,1,10]{2,1,0:T(1,128)} %bitcast.37), calls=%async_computation.6 | async-start | bytes 65536 | tf_op jit(solution)/shard_map/all_to_all | solution.py:84
  190.2 27.3 %all-to-all-start.8 = ((bf16[64,10,256]{2,1,0:T(8,128)(2,1)}), bf16[64,10,256]{2,1,0:T(8,128)(2,1)S(1)}, u32[]{:S(2)}, u32[]{:S(2)}) async-start(bf16[64,10,256]{2,1,0:T(8,128)(2,1)} %convert_element_type.235), calls=%async_computation.8 | async-start | bytes 1048576 | tf_op jit(solution)/shard_map/all_to_all | solution.py:77
  200.9 55.1 %reduce-scatter.31.cloned.1.call-start = ((), (), s32[]{:S(2)}) async-start(), calls=%async_computation.37 | async-start | bytes 655360
  238.8 21.0 %all-to-all-start.9 = ((s32[64,1,10]{2,1,0:T(1,128)}), s32[64,1,10]{2,1,0:T(1,128)S(1)}, u32[]{:S(2)}, u32[]{:S(2)}) async-start(s32[64,1,10]{2,1,0:T(1,128)} %bitcast.52), calls=%async_computation.9 | async-start | bytes 65536 | tf_op jit(solution)/shard_map/all_to_all | solution.py:84
  259.8 27.3 %all-to-all-start.11 = ((bf16[64,10,256]{2,1,0:T(8,128)(2,1)}), bf16[64,10,256]{2,1,0:T(8,128)(2,1)S(1)}, u32[]{:S(2)}, u32[]{:S(2)}) async-start(bf16[64,10,256]{2,1,0:T(8,128)(2,1)} %convert_element_type.244), calls=%async_computation.11 | async-start | bytes 1048576 | tf_op jit(solution)/shard_map/all_to_all | solution.py:77
  305.8 10.1 %all-to-all-start.13 = ((bf16[4,2,64,256]{3,2,1,0:T(8,128)(2,1)}), bf16[4,2,64,256]{3,2,1,0:T(8,128)(2,1)S(1)}, u32[]{:S(2)}, u32[]{:S(2)}) async-start(bf16[4,2,64,256]{3,2,1,0:T(8,128)(2,1)} %stack.28), calls=%async_computation.13 | async-start | bytes 524288 | tf_op jit(solution)/shard_map/all_to_all | solution.py:11
  309.2 6.7 %copy-start.4 = (bf16[5,2,64,256]{3,2,1,0:T(8,128)(2,1)S(1)}, bf16[5,2,64,256]{3,2,1,0:T(8,128)(2,1)}, u32[]{:S(2)}) copy-start(bf16[5,2,64,256]{3,2,1,0:T(8,128)(2,1)} %param.19) | copy-start | bytes 983044
  319.8 22.8 %all-to-all-start.14 = ((bf16[64,10,256]{2,1,0:T(8,128)(2,1)}), bf16[64,10,256]{2,1,0:T(8,128)(2,1)S(1)}, u32[]{:S(2)}, u32[]{:S(2)}) async-start(bf16[64,10,256]{2,1,0:T(8,128)(2,1)} %reshape.675), calls=%async_computation.14 | async-start | bytes 1048576 | tf_op jit(solution)/shard_map/all_to_all | solution.py:34
  326.0 38.4 %reduce-scatter.17.cloned.1.call-start = ((), (), s32[]{:S(2)}) async-start(), calls=%async_computation.30 | async-start | bytes 327680 | tf_op jit(solution)/shard_map/reduce_scatter | solution.py:25
  342.7 1.2 copy-start.2
  365.9 10.1 %all-to-all-start.15 = ((bf16[4,2,64,256]{3,2,1,0:T(8,128)(2,1)}), bf16[4,2,64,256]{3,2,1,0:T(8,128)(2,1)S(1)}, u32[]{:S(2)}, u32[]{:S(2)}) async-start(bf16[4,2,64,256]{3,2,1,0:T(8,128)(2,1)} %stack.29), calls=%async_computation.16 | async-start | bytes 524288 | tf_op jit(solution)/shard_map/all_to_all | solution.py:11
  379.8 27.3 %all-to-all-start.16 = ((bf16[64,10,256]{2,1,0:T(8,128)(2,1)}), bf16[64,10,256]{2,1,0:T(8,128)(2,1)S(1)}, u32[]{:S(2)}, u32[]{:S(2)}) async-start(bf16[64,10,256]{2,1,0:T(8,128)(2,1)} %reshape.681), calls=%async_computation.17 | async-start | bytes 1048576 | tf_op jit(solution)/shard_map/all_to_all | solution.py:34
  390.4 38.3 %reduce-scatter.19.cloned.1.call-start = ((), (), s32[]{:S(2)}) async-start(), calls=%async_computation.31 | async-start | bytes 327680 | tf_op jit(solution)/shard_map/reduce_scatter | solution.py:25
  430.3 10.1 %all-to-all-start.17 = ((bf16[4,2,64,256]{3,2,1,0:T(8,128)(2,1)}), bf16[4,2,64,256]{3,2,1,0:T(8,128)(2,1)S(1)}, u32[]{:S(2)}, u32[]{:S(2)}) async-start(bf16[4,2,64,256]{3,2,1,0:T(8,128)(2,1)} %stack.30), calls=%async_computation.19 | async-start | bytes 524288 | tf_op jit(solution)/shard_map/all_to_all | solution.py:11
  444.3 27.2 %all-to-all-start.18 = ((bf16[64,10,256]{2,1,0:T(8,128)(2,1)}), bf16[64,10,256]{2,1,0:T(8,128)(2,1)S(1)}, u32[]{:S(2)}, u32[]{:S(2)}) async-start(bf16[64,10,256]{2,1,0:T(8,128)(2,1)} %reshape.687), calls=%async_computation.20 | async-start | bytes 1048576 | tf_op jit(solution)/shard_map/all_to_all | solution.py:34
  454.9 38.3 %reduce-scatter.21.cloned.1.call-start = ((), (), s32[]{:S(2)}) async-start(), calls=%async_computation.32 | async-start | bytes 327680 | tf_op jit(solution)/shard_map/reduce_scatter | solution.py:25
  494.8 10.1 %all-to-all-start.19 = ((bf16[4,2,64,256]{3,2,1,0:T(8,128)(2,1)}), bf16[4,2,64,256]{3,2,1,0:T(8,128)(2,1)S(1)}, u32[]{:S(2)}, u32[]{:S(2)}) async-start(bf16[4,2,64,256]{3,2,1,0:T(8,128)(2,1)} %stack.31), calls=%async_computation.22 | async-start | bytes 524288 | tf_op jit(solution)/shard_map/all_to_all | solution.py:11
  508.7 27.2 %all-to-all-start.20 = ((bf16[64,10,256]{2,1,0:T(8,128)(2,1)}), bf16[64,10,256]{2,1,0:T(8,128)(2,1)S(1)}, u32[]{:S(2)}, u32[]{:S(2)}) async-start(bf16[64,10,256]{2,1,0:T(8,128)(2,1)} %reshape.693), calls=%async_computation.23 | async-start | bytes 1048576 | tf_op jit(solution)/shard_map/all_to_all | solution.py:34
  519.3 38.3 %reduce-scatter.23.cloned.1.call-start = ((), (), s32[]{:S(2)}) async-start(), calls=%async_computation.33 | async-start | bytes 327680 | tf_op jit(solution)/shard_map/reduce_scatter | solution.py:25
  567.9 0.7 copy-start
Sparse Core Ops, SparseCore 0:
  21.7 25.1 reduce-scatter.24
  97.5 19.0 reduce-scatter.26
  167.1 19.1 reduce-scatter.28
  236.8 19.1 reduce-scatter.30
  345.1 19.1 reduce-scatter.16
  409.6 19.1 reduce-scatter.18
  474.0 19.1 reduce-scatter.20
  538.4 19.1 reduce-scatter.22
